TPU v7x, 32 devices: a whole 2x2x4 slice. The times are simulated.
32 devices in a mesh: ka: 16 (over z, y, core), aux: 2 (over x).
Axes of the slice: x: 2, y: 2, z: 4, core: 2. Of those that a mesh axis runs over, the one named last changes fastest.
Arguments:
- coefficients: bfloat16 [16, 4096, 128], P('ka'), may hold values from -2.09375 to 2.09375
- triple: bfloat16 [64, 2, 64, 768], P('aux'), may hold values from -0.5 to 0.5
- neighbors: int32 [64, 2], P('aux'), may hold values from 0 to 63
- w_screened: bfloat16 [16, 768, 1536], P('ka', 'aux'), as said below
- partner: int32 [2, 16], replicated, may hold values from 0 to 15, each once within a row
- q_ids: int32 [2], replicated, may hold values from 0 to 15
Outputs:
- sigma: float32 [16, 64, 128], P('ka', 'aux')
Inputs may be any that keep to these rules, and one draw needn't show every extreme that they name: Each stored w_screened is Hermitian: its real block is symmetric and its imaginary block antisymmetric.
All inputs are finite; a program needn't handle non-finite values.
Results may differ from a plain program's by a relative error of at most 0.0085.
Values may be sent and summed in bfloat16 or wider, within the bound.
A program may use at most 128 MiB of HBM per device.

v0:
```python
import math
import jax
import jax.numpy as jnp
from jax import lax
from jax.sharding import PartitionSpec as P

CELL_ATOMS = 64
ORBITALS_PER_ATOM = 64
AUX_ATOM = 12
OCCUPIED_BANDS = 16
TRANSFERS = 2
NAUX = 768


def from_root(block, axis, source):
    block = jnp.where(lax.axis_index(axis) == source, block, jnp.zeros_like(block))
    return lax.psum(block, axis)


def from_partner(value, axis, distance):
    mask = 2**distance
    pairs = [(source, source ^ mask) for source in range(lax.axis_size(axis))]
    return lax.ppermute(value, axis, pairs)


def rotated_parts(values, band_count):
    return jnp.concatenate([-values[..., band_count:], values[..., :band_count]], axis=-1)


def apply_block(weights, start, values, band_count):
    kpoints, rows, occupied, doubled = values.shape
    real_cols = lax.dynamic_slice_in_dim(weights, start, rows, 1)
    imag_cols = lax.dynamic_slice_in_dim(weights, NAUX + start, rows, 1)
    flat = values.reshape(kpoints, rows, occupied * doubled)
    turned = rotated_parts(values, band_count).reshape(kpoints, rows, occupied * doubled)
    result = jnp.einsum("ab,kbx->kax", real_cols, flat, preferred_element_type=jnp.float32)
    result = result + jnp.einsum(
        "ab,kbx->kax", imag_cols, turned, preferred_element_type=jnp.float32
    )
    return result.reshape(kpoints, weights.shape[0], occupied, doubled)


def pair_blocks(left_values, right_values):
    kpoints = left_values.shape[0]
    doubled = left_values.shape[-1]
    left_flat = left_values.reshape(kpoints, -1, doubled)
    right_flat = right_values.reshape(kpoints, -1, doubled)
    return jnp.einsum("kxm,kxn->kmn", left_flat, right_flat, preferred_element_type=jnp.float32)


def sigma_parts(blocks, band_count):
    sigma_real = blocks[:, :band_count, :band_count] + blocks[:, band_count:, band_count:]
    sigma_imag = blocks[:, :band_count, band_count:] - blocks[:, band_count:, :band_count]
    return (sigma_real, sigma_imag)


def local(coefficients, triple, neighbors, w_screened, partner, q_ids):
    kpoints, orbitals, doubled = coefficients.shape
    band_count = doubled // 2
    local_atoms = triple.shape[0]
    local_aux = local_atoms * AUX_ATOM
    half_index = lax.axis_index("aux")
    prefactor = -1.0 / math.sqrt(TRANSFERS * NAUX * OCCUPIED_BANDS)
    screens = [
        from_root(w_screened[0], "ka", q_ids[momentum_transfer])
        for momentum_transfer in range(TRANSFERS)
    ]
    far_cols = jnp.concatenate(
        [
            coefficients[:, :, :OCCUPIED_BANDS],
            coefficients[:, :, band_count : band_count + OCCUPIED_BANDS],
        ],
        axis=2,
    )
    packed = far_cols.reshape(kpoints, orbitals * 2 * OCCUPIED_BANDS // 128, 128)
    spread = lax.all_to_all(packed, "ka", split_axis=1, concat_axis=0, tiled=True)
    permuted = jnp.take(spread, partner, axis=0)
    arrived = jnp.stack(
        [
            lax.all_to_all(
                permuted[momentum_transfer], "ka", split_axis=0, concat_axis=1, tiled=True
            )
            for momentum_transfer in range(TRANSFERS)
        ]
    )
    distant_coefficients = arrived.reshape(
        TRANSFERS, kpoints, CELL_ATOMS, ORBITALS_PER_ATOM, 2 * OCCUPIED_BANDS
    )
    own_rows = lax.dynamic_slice_in_dim(
        coefficients,
        half_index * local_atoms * ORBITALS_PER_ATOM,
        local_atoms * ORBITALS_PER_ATOM,
        1,
    )
    home_coefficients = own_rows.reshape(kpoints, local_atoms, ORBITALS_PER_ATOM, doubled)
    neighbour_coef = jnp.take(distant_coefficients, neighbors, axis=2)
    pair_half = jnp.einsum(
        "tkcjoy,cjox->tkcyx", neighbour_coef, triple, preferred_element_type=jnp.float32
    ).astype(jnp.bfloat16)
    pair_half = pair_half.reshape(
        TRANSFERS, kpoints, local_atoms, 2 * OCCUPIED_BANDS, AUX_ATOM, ORBITALS_PER_ATOM
    )
    combos = jnp.einsum(
        "kcix,tkcyai->tkcayx", home_coefficients, pair_half, preferred_element_type=jnp.float32
    )
    real_part = (
        combos[..., :OCCUPIED_BANDS, :band_count] + combos[..., OCCUPIED_BANDS:, band_count:]
    )
    imag_part = (
        combos[..., OCCUPIED_BANDS:, :band_count] - combos[..., :OCCUPIED_BANDS, band_count:]
    )
    products = jnp.concatenate([real_part, imag_part], axis=-1).astype(jnp.bfloat16)
    products = products.reshape(TRANSFERS, kpoints, local_aux, OCCUPIED_BANDS, doubled)
    pairs = products.reshape(TRANSFERS // 2, 2, kpoints, local_aux, OCCUPIED_BANDS, doubled)
    screen_pairs = jnp.stack(screens).reshape(TRANSFERS // 2, 2, local_aux, 2 * NAUX)
    outgoing = lax.dynamic_index_in_dim(pairs, 1 - half_index, 1, keepdims=False)
    incoming = from_partner(outgoing, "aux", 0)
    own_start = half_index * local_aux
    other_start = (1 - half_index) * local_aux
    full_weights = lax.dynamic_index_in_dim(screen_pairs[0], half_index, 0, keepdims=False)
    part_weights = lax.dynamic_index_in_dim(screen_pairs[0], 1 - half_index, 0, keepdims=False)
    full_values = lax.dynamic_index_in_dim(pairs[0], half_index, 0, keepdims=False)
    part_values = lax.dynamic_index_in_dim(pairs[0], 1 - half_index, 0, keepdims=False)
    cross = apply_block(full_weights, other_start, incoming[0], band_count)
    full_screened = (apply_block(full_weights, own_start, full_values, band_count) + cross).astype(
        jnp.bfloat16
    )
    part_screened = apply_block(part_weights, own_start, part_values, band_count).astype(
        jnp.bfloat16
    )
    cross_screened = cross.astype(jnp.bfloat16)
    diagonal = pair_blocks(full_values, full_screened) + pair_blocks(part_values, part_screened)
    diag_real, diag_imag = sigma_parts(diagonal, band_count)
    cross_real, cross_imag = sigma_parts(pair_blocks(full_values, cross_screened), band_count)
    total_real = diag_real + jnp.transpose(cross_real, (0, 2, 1))
    total_imag = diag_imag - jnp.transpose(cross_imag, (0, 2, 1))
    local_sigma = jnp.concatenate([total_real, total_imag], axis=-1)
    local_sigma = prefactor * local_sigma
    return lax.psum_scatter(
        local_sigma.astype(jnp.bfloat16), "aux", scatter_dimension=1, tiled=True
    ).astype(jnp.float32)


def solution(mesh):
    in_specs = (
        P("ka", None, None),
        P("aux", None, None, None),
        P("aux", None),
        P("ka", "aux", None),
        P(),
        P(),
    )
    out_specs = P("ka", "aux", None)
    return jax.shard_map(local, mesh=mesh, in_specs=in_specs, out_specs=out_specs, check_vma=False)
```

profile of v0, /device:TPU:0, one launch (start us, length us, event | category | flops | bytes accessed | tf_op | source)
XLA Modules:
  0.0 210.7 jit_solution(5651449956877544662)
XLA Ops:
  6.5 2.1 fusion.62
  10.9 2.2 %reduce = bf16[1024,128]{1,0:T(8,128)(2,1)S(1)} reduce(bf16[1024,1,128]{2,1,0:T(2,128)(2,1)S(1)} %bitcast.159, bf16[]{:T(256)} %broadcast.52), dimensions={1}, to_apply=%bitcast.134.reduce_sub_computation | reduce | bytes 524290
  13.1 0.8 reshape.297
  13.9 7.4 %all-to-all-start = ((bf16[16,2,4096]{2,1,0:T(2,128)(2,1)}), bf16[16,2,4096]{2,1,0:T(2,128)(2,1)S(1)}, u32[]{:S(2)}, u32[]{:S(2)}) async-start(bf16[16,2,4096]{2,1,0:T(2,128)(2,1)} %reshape.297), calls=%async_computation | async-start | bytes 524288 | tf_op jit(solution)/shard_map/all_to_all | solution.py:76
  23.3 8.0 %all-to-all-done = bf16[16,2,4096]{2,1,0:T(2,128)(2,1)S(1)} async-done(((bf16[16,2,4096]{2,1,0:T(2,128)(2,1)}), bf16[16,2,4096]{2,1,0:T(2,128)(2,1)S(1)}, u32[]{:S(2)}, u32[]{:S(2)}) %all-to-all-start) | async-done | bytes 262176 | tf_op jit(solution)/shard_map/all_to_all | solution.py:76
  32.4 0.8 slice_bitcast_fusion.1
  33.3 3.5 %all-to-all-start.1 = ((bf16[16,64,128]{2,1,0:T(8,128)(2,1)}), bf16[16,64,128]{2,1,0:T(8,128)(2,1)S(1)}, u32[]{:S(2)}, u32[]{:S(2)}) async-start(bf16[16,64,128]{2,1,0:T(8,128)(2,1)} %get-tuple-element.21), calls=%async_computation.1 | async-start | bytes 524288 | tf_op jit(solution)/shard_map/all_to_all | solution.py:80
  36.9 1.6 broadcast_select_fusion
  39.3 7.4 %all-to-all-done.1 = bf16[16,64,128]{2,1,0:T(8,128)(2,1)S(1)} async-done(((bf16[16,64,128]{2,1,0:T(8,128)(2,1)}), bf16[16,64,128]{2,1,0:T(8,128)(2,1)S(1)}, u32[]{:S(2)}, u32[]{:S(2)}) %all-to-all-start.1) | async-done | bytes 262176 | tf_op jit(solution)/shard_map/all_to_all | solution.py:80
  46.8 3.5 %all-to-all-start.2 = ((bf16[16,64,128]{2,1,0:T(8,128)(2,1)}), bf16[16,64,128]{2,1,0:T(8,128)(2,1)S(1)}, u32[]{:S(2)}, u32[]{:S(2)}) async-start(bf16[16,64,128]{2,1,0:T(8,128)(2,1)} %get-tuple-element.22), calls=%async_computation.2 | async-start | bytes 524288 | tf_op jit(solution)/shard_map/all_to_all | solution.py:80
  50.7 0.8 constant_dynamic-slice_fusion
  52.0 11.2 %all-to-all-done.2 = bf16[16,64,128]{2,1,0:T(8,128)(2,1)S(1)} async-done(((bf16[16,64,128]{2,1,0:T(8,128)(2,1)}), bf16[16,64,128]{2,1,0:T(8,128)(2,1)S(1)}, u32[]{:S(2)}, u32[]{:S(2)}) %all-to-all-start.2) | async-done | bytes 262176 | tf_op jit(solution)/shard_map/all_to_all | solution.py:80
  63.1 1.4 stack.19
  64.5 1.7 maximum_bitcast_fusion
  66.2 2.1 %gather_fusion.1 = bf16[64,2,64,32]{3,2,1,0:T(8,128)(2,1)} fusion(bf16[2,64,64,32]{3,2,1,0:T(8,128)(2,1)S(1)} %maximum_bitcast_fusion, s32[1024]{0:T(1024)S(1)} %pad_clamp_fusion), kind=kCustom, calls=%fused_computation.1 | custom fusion | bytes 1048832 | tf_op jit(solution)/shard_map/jit(_take)/gather | solution.py:96
  68.4 2.8 %copy.46 = bf16[64,2,64,32]{2,3,1,0:T(8,128)(2,1)} copy(bf16[64,2,64,32]{3,2,1,0:T(8,128)(2,1)} %gather_fusion.1) | data formatting | bytes 1048576 | tf_op jit(solution)/shard_map/jit(_take)/gather | solution.py:96
  71.1 4.9 %fusion.9 = bf16[2,1,32,32,768]{4,3,0,2,1:T(8,128)(2,1)S(1)} fusion(bf16[32,2,64,768]{3,2,1,0:T(8,128)(2,1)} %param.7, bf16[32,2,2,64,32]{3,4,2,1,0:T(8,128)(2,1)} %bitcast.155, pred[32,2]{1,0:T(8,128)(4,1)S(1)} %copy.40), kind=kOutput, calls=%fused_computation.12 | convolution fusion | flops 404488192 | bytes 9961536 | tf_op jit(solution)/shard_map/tkcjoy,cjox->tkcyx/dot_general | solution.py:97
  76.0 7.2 %reshape.296 = bf16[2,32,32,12,64]{4,3,2,0,1:T(8,128)(2,1)} reshape(bf16[2,1,32,32,768]{4,3,0,2,1:T(8,128)(2,1)S(1)} %fusion.9) | data formatting | bytes 6291456 | tf_op jit(solution)/shard_map/reshape.12
  83.2 5.1 %fusion.6 = f32[2,1,32,12,32,128]{5,4,3,0,2,1:T(8,128)S(1)} fusion(bf16[32,64,128,1,1]{2,1,4,3,0:T(8,128)(2,1)} %bitcast.160, bf16[2,32,32,12,64]{4,3,2,0,1:T(8,128)(2,1)} %reshape.296), kind=kOutput, calls=%fused_computation.11 | convolution fusion | flops 402653184 | bytes 16252928 | tf_op jit(solution)/shard_map/kcix,tkcyai->tkcayx/dot_general | solution.py:103
  88.3 3.7 %fusion = (bf16[2,1,32,12,16,64]{5,4,3,0,2,1:T(8,128)(2,1)S(1)}, bf16[2,1,32,12,16,64]{5,4,3,0,2,1:T(8,128)(2,1)S(1)}) fusion(f32[2,1,32,12,32,128]{5,4,3,0,2,1:T(8,128)S(1)} %fusion.6), kind=kLoop, calls=%fused_computation.3 | loop fusion | flops 3145728 | bytes 15728640 | tf_op jit(solution)/shard_map/convert.6
  93.3 2.1 fusion.17
  95.4 1.6 collective-permute-start
  97.0 1.7 fusion.14
  99.3 2.0 pad_maximum_fusion.2
  102.0 2.1 %pad_maximum_fusion = bf16[1,384,16,128]{3,2,1,0:T(8,128)(2,1)} fusion(bf16[1,384,16,64]{3,2,1,0:T(8,128)(2,1)S(1)} %get-tuple-element.14, bf16[1,384,16,64]{3,2,1,0:T(8,128)(2,1)S(1)} %get-tuple-element.13), kind=kLoop, calls=%fused_computation.47 | loop fusion | flops 3145728 | bytes 3145728 | tf_op jit(solution)/shard_map/concatenate | solution.py:27
  104.1 42.1 %all-reduce.3.cloned.1.call-done = (bf16[1,384,1536]{2,1,0:T(8,128)(2,1)}, bf16[1,384,1536]{2,1,0:T(8,128)(2,1)}) async-done(((bf16[1,384,1536]{2,1,0:T(8,128)(2,1)}, bf16[1,384,1536]{2,1,0:T(8,128)(2,1)}), (bf16[1,384,1536]{2,1,0:T(8,128)(2,1)}, bf16[1,384,1536]{2,1,0:T(8,128)(2,1)})) %all-reduce.3.cloned.1.call-update) | async-done | bytes 2359312 | tf_op jit(solution)/shard_map/psum | solution.py:17
  146.2 1.4 constant_dynamic-update-slice_fusion.1
  148.0 1.3 fusion.20
  149.3 0.9 copy-done.4
  150.2 2.5 %fusion.11 = bf16[1,384,2048]{1,2,0:T(8,128)(2,1)} fusion(f32[2048,384]{1,0:T(8,128)S(1)} %fusion.20, bf16[48,8,16,128]{3,2,1,0:T(8,128)(2,1)S(1)} %bitcast.157, bf16[2,384,1536]{2,1,0:T(8,128)(2,1)S(1)} %constant_dynamic-update-slice_fusion, s32[]{:T(128)S(6)} %select_n.104, s32[]{:T(128)S(6)} %select_n.98), kind=kOutput, calls=%fused_computation.23 | convolution fusion | flops 605552640 | bytes 6586376 | tf_op jit(solution)/shard_map/ab,kbx->kax/dot_general | solution.py:37
  152.7 2.6 %copy.55 = bf16[1,384,2048]{2,1,0:T(8,128)(2,1)} copy(bf16[1,384,2048]{1,2,0:T(8,128)(2,1)} %fusion.11) | data formatting | bytes 3145728 | tf_op jit(solution)/shard_map/convert_element_type | solution.py:128
  155.3 3.7 %convert_element_type.101 = bf16[6144,128]{1,0:T(8,128)(2,1)} reshape(bf16[1,384,2048]{2,1,0:T(8,128)(2,1)} %copy.55) | data formatting | bytes 3145728 | tf_op jit(solution)/shard_map/convert_element_type | solution.py:128
  159.1 2.3 %fusion.30 = f32[2048,384]{1,0:T(8,128)S(1)} fusion(bf16[48,8,16,128]{3,2,1,0:T(8,128)(2,1)S(1)} %bitcast.144, bf16[2,384,1536]{2,1,0:T(8,128)(2,1)} %copy-done.5, s32[]{:T(128)S(6)} %select_n.94, s32[]{:T(128)S(6)} %select_n.96), kind=kOutput, calls=%fused_computation.41 | convolution fusion | flops 603979776 | bytes 5013512 | tf_op jit(solution)/shard_map/ab,kbx->kax/dot_general | solution.py:36
  161.3 2.6 %slice_negate_fusion.1 = (bf16[1,384,16,64]{3,2,1,0:T(8,128)(2,1)S(1)}, bf16[1,384,16,64]{3,2,1,0:T(8,128)(2,1)S(1)}) fusion(bf16[1,384,16,128]{3,2,1,0:T(8,128)(2,1)} %bitcast.31), kind=kLoop, calls=%fused_computation.45 | loop fusion | flops 393216 | bytes 3145728 | tf_op jit(solution)/shard_map/neg | solution.py:27
  163.9 0.9 pad_maximum_fusion.1
  164.8 2.2 %fusion.23 = f32[2048,384]{1,0:T(8,128)S(1)} fusion(bf16[48,8,16,128]{3,2,1,0:T(8,128)(2,1)S(1)} %bitcast.154, bf16[2,384,1536]{2,1,0:T(8,128)(2,1)} %copy-done.5, s32[]{:T(128)S(6)} %select_n.94, s32[]{:T(128)S(6)} %select_n.103), kind=kOutput, calls=%fused_computation.34 | convolution fusion | flops 603979776 | bytes 5013512 | tf_op jit(solution)/shard_map/ab,kbx->kax/dot_general | solution.py:37
  167.0 2.8 %convolution_add_fusion = f32[2048,384]{1,0:T(8,128)S(1)} fusion(f32[2048,384]{1,0:T(8,128)S(1)} %fusion.23, bf16[48,8,16,128]{3,2,1,0:T(8,128)(2,1)} %bitcast.70, bf16[2,384,1536]{2,1,0:T(8,128)(2,1)} %copy-done.5, s32[]{:T(128)S(6)} %select_n.94, s32[]{:T(128)S(6)} %select_n.101), kind=kOutput, calls=%fused_computation.17 | convolution fusion | flops 604766208 | bytes 8159240 | tf_op jit(solution)/shard_map/ab,kbx->kax/dot_general | solution.py:36
  169.8 1.3 convert_bitcast_fusion
  171.8 3.6 %fusion.10 = bf16[1,384,2048]{1,2,0:T(8,128)(2,1)} fusion(f32[2048,384]{1,0:T(8,128)S(1)} %convolution_add_fusion, f32[2048,384]{1,0:T(8,128)S(1)} %fusion.30, bf16[48,8,16,128]{3,2,1,0:T(8,128)(2,1)S(1)} %bitcast.156, bf16[2,384,1536]{2,1,0:T(8,128)(2,1)} %copy-done.5, s32[]{:T(128)S(6)} %select_n.94, s32[]{:T(128)S(6)} %select_n.98), kind=kOutput, calls=%fused_computation.22 | convolution fusion | flops 606339072 | bytes 9732104 | tf_op jit(solution)/shard_map/ab,kbx->kax/dot_general | solution.py:37
  175.4 2.7 %copy.54 = bf16[1,384,2048]{2,1,0:T(8,128)(2,1)} copy(bf16[1,384,2048]{1,2,0:T(8,128)(2,1)} %fusion.10) | data formatting | bytes 3145728 | tf_op jit(solution)/shard_map/convert_element_type | solution.py:125
  178.1 3.7 %convert_element_type.97 = bf16[6144,128]{1,0:T(8,128)(2,1)} reshape(bf16[1,384,2048]{2,1,0:T(8,128)(2,1)} %copy.54) | data formatting | bytes 3145728 | tf_op jit(solution)/shard_map/convert_element_type | solution.py:125
  181.8 2.6 %copy.56 = bf16[1,384,2048]{2,1,0:T(8,128)(2,1)} copy(bf16[1,384,2048]{1,2,0:T(8,128)(2,1)} %convert_bitcast_fusion) | data formatting | bytes 3145728 | tf_op jit(solution)/shard_map/convert_element_type | solution.py:131
  184.4 3.7 %convert_element_type.105 = bf16[6144,128]{1,0:T(8,128)(2,1)} reshape(bf16[1,384,2048]{2,1,0:T(8,128)(2,1)} %copy.56) | data formatting | bytes 3145728 | tf_op jit(solution)/shard_map/convert_element_type | solution.py:131
  188.2 2.1 %fusion.64 = f32[128,128]{1,0:T(8,128)S(1)} fusion(bf16[6144,128]{1,0:T(8,128)(2,1)S(1)} %bitcast.145, bf16[6144,128]{1,0:T(8,128)(2,1)} %convert_element_type.97), kind=kOutput, calls=%fused_computation.104 | convolution fusion | flops 201326592 | bytes 3211264 | tf_op jit(solution)/shard_map/kxm,kxn->kmn/dot_general | solution.py:48
  191.0 0.8 copy-done.2
  192.5 0.7 fusion.54
  193.2 9.4 %reduce-scatter.2.cloned.1.call-done = bf16[1,32,128]{2,1,0:T(8,128)(2,1)} async-done(((bf16[1,64,128]{2,1,0:T(8,128)(2,1)}), bf16[1,32,128]{2,1,0:T(8,128)(2,1)}) %reduce-scatter.2.cloned.1.call-update) | async-done | bytes 8208 | tf_op jit(solution)/shard_map/reduce_scatter | solution.py:139
  202.6 1.3 convert_element_type.107
  (55 shorter events, 10.6 us)
Async XLA Ops:
  9.7 11.6 %copy-start.9 = (s32[2,16]{1,0:T(2,128)S(1)}, s32[2,16]{1,0:T(2,128)}, u32[]{:S(2)}) copy-start(s32[2,16]{1,0:T(2,128)} %param.10) | copy-start | bytes 388
  9.8 11.7 %copy-start.8 = (s32[2]{0:T(128)S(1)}, s32[2]{0:T(128)}, u32[]{:S(2)}) copy-start(s32[2]{0:T(128)} %param.11) | copy-start | bytes 28
  13.9 17.4 %all-to-all-start = ((bf16[16,2,4096]{2,1,0:T(2,128)(2,1)}), bf16[16,2,4096]{2,1,0:T(2,128)(2,1)S(1)}, u32[]{:S(2)}, u32[]{:S(2)}) async-start(bf16[16,2,4096]{2,1,0:T(2,128)(2,1)} %reshape.297), calls=%async_computation | async-start | bytes 524288 | tf_op jit(solution)/shard_map/all_to_all | solution.py:76
  32.3 4.6 %copy-start.7 = (bf16[1,384,1536]{2,1,0:T(8,128)(2,1)S(1)}, bf16[1,384,1536]{2,1,0:T(8,128)(2,1)}, u32[]{:S(2)}) copy-start(bf16[1,384,1536]{2,1,0:T(8,128)(2,1)} %param.9) | copy-start | bytes 3538948
  33.3 13.5 %all-to-all-start.1 = ((bf16[16,64,128]{2,1,0:T(8,128)(2,1)}), bf16[16,64,128]{2,1,0:T(8,128)(2,1)S(1)}, u32[]{:S(2)}, u32[]{:S(2)}) async-start(bf16[16,64,128]{2,1,0:T(8,128)(2,1)} %get-tuple-element.21), calls=%async_computation.1 | async-start | bytes 524288 | tf_op jit(solution)/shard_map/all_to_all | solution.py:80
  36.8 109.4 %all-reduce.3.cloned.1.call-start = ((), (), s32[]{:S(2)}) async-start(), calls=%async_computation.5 | async-start | bytes 4718592 | tf_op jit(solution)/shard_map/psum | solution.py:17
  38.5 0.7 copy-start.10
  38.5 12.2 %copy-start = (bf16[1,4096,128]{2,1,0:T(8,128)(2,1)S(1)}, bf16[1,4096,128]{2,1,0:T(8,128)(2,1)}, u32[]{:S(2)}) copy-start(bf16[1,4096,128]{2,1,0:T(8,128)(2,1)} %param.6) | copy-start | bytes 3145732
  46.8 16.4 %all-to-all-start.2 = ((bf16[16,64,128]{2,1,0:T(8,128)(2,1)}), bf16[16,64,128]{2,1,0:T(8,128)(2,1)S(1)}, u32[]{:S(2)}, u32[]{:S(2)}) async-start(bf16[16,64,128]{2,1,0:T(8,128)(2,1)} %get-tuple-element.22), calls=%async_computation.2 | async-start | bytes 524288 | tf_op jit(solution)/shard_map/all_to_all | solution.py:80
  50.3 152.2 %reduce-scatter.2.cloned.1.call-start = ((), (), s32[]{:S(2)}) async-start(), calls=%async_computation.4 | async-start | bytes 24576 | tf_op jit(solution)/shard_map/reduce_scatter | solution.py:139
  95.4 65.9 %collective-permute-start = (bf16[1,1,384,16,128]{4,3,2,1,0:T(8,128)(2,1)}, bf16[1,1,384,16,128]{4,3,2,1,0:T(8,128)(2,1)}, u32[]{:S(2)}, u32[]{:S(2)}) collective-permute-start(bf16[1,1,384,16,128]{4,3,2,1,0:T(8,128)(2,1)} %fusion.17), channel_id=1, source_target_pairs={{0,1},{1,0},{2,3},{3,2},{4,5},{5,4},{6,7},{7,6},{8,9},{9,8},{10,11... | collective-permute-start | bytes 4718600 | tf_op jit(solution)/shard_map/ppermute | solution.py:23
  146.2 1.6 copy-start.6
  147.9 1.4 copy-start.5
  147.9 2.3 %copy-start.4 = (bf16[1,384,16,128]{3,2,1,0:T(8,128)(2,1)S(1)}, bf16[1,384,16,128]{3,2,1,0:T(8,128)(2,1)}, u32[]{:S(2)}) copy-start(bf16[1,384,16,128]{3,2,1,0:T(8,128)(2,1)} %pad_maximum_fusion.2) | copy-start | bytes 4718596
  169.8 2.0 copy-start.1
  188.2 2.1 %copy-start.3 = (bf16[6144,128]{1,0:T(8,128)(2,1)S(1)}, bf16[6144,128]{1,0:T(8,128)(2,1)}, u32[]{:S(2)}) copy-start(bf16[6144,128]{1,0:T(8,128)(2,1)} %convert_element_type.105) | copy-start | bytes 4718596
  190.3 1.4 copy-start.2
Sparse Core Ops, SparseCore 0:
  41.2 104.9 all-reduce.2
  193.3 9.2 reduce-scatter.1
where the time goes:
time: 212 us; the launch traced here: 211 us
  waiting for transfers between devices  78.2 us (37%)
  local copies, waits for them, and re-layouts  47.6 us (22%)
  matrix products  28.1 us (13%)
  other arithmetic  25.5 us (12%)
  starting transfers between devices  16.3 us (8%)
  between operations  15.1 us (7%)
    psum x1, waiting for transfers between devices, from_root(): return lax.psum(block, axis)  42.1 us
    all_to_all x2, waiting for transfers between devices, local(): lax.all_to_all(permuted[momentum_transfer], 'ka', split_axis=0, concat_ax...  18.6 us
    reduce_scatter x1, waiting for transfers between devices, local(): lax.psum_scatter(local_sigma.astype(jnp.bfloat16), 'aux', scatter_dimensi...  9.4 us
    another operation x3, local copies, waits for them, and re-layouts  8.42 us
    dot_general x3, matrix products, apply_block(): jnp.einsum('ab,kbx->kax', imag_cols, turned, preferred_element_type=jnp.f...  8.36 us
    all_to_all x1, waiting for transfers between devices, local(): lax.all_to_all(packed, 'ka', split_axis=1, concat_axis=0, tiled=True)  8.01 us
    all_to_all x1, starting transfers between devices, local(): lax.all_to_all(packed, 'ka', split_axis=1, concat_axis=0, tiled=True)  7.41 us
    all_to_all x2, starting transfers between devices, local(): lax.all_to_all(permuted[momentum_transfer], 'ka', split_axis=0, concat_ax...  7.06 us
  transfers between devices with their start and end apart: 6, of which 5 were waited for; matrix products, arithmetic and copies ran while one was open for 27% of the time, Pallas kernels for 0%

commit v1 on v0

--- a/solution.py
+++ b/solution.py
@@ -10,6 +10,12 @@
 OCCUPIED_BANDS = 16
 TRANSFERS = 2
 NAUX = 768
+
+
+def exchange_blocks(shard, name, split, join):
+    pieces = jnp.split(shard, lax.axis_size(name), axis=split)
+    received = lax.all_to_all(jnp.stack(pieces), name, 0, 0)
+    return jnp.concatenate(received, axis=join)
 
 
 def from_root(block, axis, source):
@@ -77,9 +83,7 @@
     permuted = jnp.take(spread, partner, axis=0)
     arrived = jnp.stack(
         [
-            lax.all_to_all(
-                permuted[momentum_transfer], "ka", split_axis=0, concat_axis=1, tiled=True
-            )
+            exchange_blocks(permuted[momentum_transfer], "ka", 0, 1)
             for momentum_transfer in range(TRANSFERS)
         ]
     )

time: 212 us -> 221 us (1.042)
  local copies, waits for them, and re-layouts: 47.6 us -> 56.6 us
    unnamed x29 -> x44, local copies, waits for them, and re-layouts: 6.87 us -> 16 us
    another operation x5 -> x6, local copies, waits for them, and re-layouts: 10.2 us -> 10.9 us
  transfers between devices with their start and end apart: 6 -> 6, of which waited for: 5 -> 5; matrix products, arithmetic and copies ran while one was open for 27% -> 26% of each run, Pallas kernels for 0% -> 0%
where the time goes in v1:
time: 221 us; the launch traced here: 220 us
  waiting for transfers between devices  78.1 us (35%)
  local copies, waits for them, and re-layouts  56.6 us (26%)
  matrix products  28 us (13%)
  other arithmetic  25.6 us (12%)
  starting transfers between devices  16.3 us (7%)
  between operations  15.1 us (7%)
    psum x1, waiting for transfers between devices, from_root(): return lax.psum(block, axis)  42.1 us
    all_to_all x2, waiting for transfers between devices, exchange_blocks(): received = lax.all_to_all(jnp.stack(pieces), name, 0, 0)  18.5 us
    unnamed x44, local copies, waits for them, and re-layouts  16 us
    reduce_scatter x1, waiting for transfers between devices, local(): lax.psum_scatter(local_sigma.astype(jnp.bfloat16), 'aux', scatter_dimensi...  9.4 us
    another operation x3, local copies, waits for them, and re-layouts  8.44 us
    dot_general x3, matrix products, apply_block(): jnp.einsum('ab,kbx->kax', imag_cols, turned, preferred_element_type=jnp.f...  8.31 us
    all_to_all x1, waiting for transfers between devices, local(): lax.all_to_all(packed, 'ka', split_axis=1, concat_axis=0, tiled=True)  8 us
    all_to_all x1, starting transfers between devices, local(): lax.all_to_all(packed, 'ka', split_axis=1, concat_axis=0, tiled=True)  7.41 us
  transfers between devices with their start and end apart: 6, of which 5 were waited for; matrix products, arithmetic and copies ran while one was open for 26% of the time, Pallas kernels for 0%

profile of v1, /device:TPU:0, one launch (start us, length us, event | category | flops | bytes accessed | tf_op | source)
XLA Modules:
  0.0 219.8 jit_solution(2579364950900360831)
XLA Ops:
  6.5 2.1 fusion.62
  10.9 2.2 %reduce = bf16[1024,128]{1,0:T(8,128)(2,1)S(1)} reduce(bf16[1024,1,128]{2,1,0:T(2,128)(2,1)S(1)} %bitcast.159, bf16[]{:T(256)} %broadcast.52), dimensions={1}, to_apply=%bitcast.134.reduce_sub_computation | reduce | bytes 524290
  13.1 0.8 reshape.353
  13.9 7.4 %all-to-all-start = ((bf16[16,2,4096]{2,1,0:T(2,128)(2,1)}), bf16[16,2,4096]{2,1,0:T(2,128)(2,1)S(1)}, u32[]{:S(2)}, u32[]{:S(2)}) async-start(bf16[16,2,4096]{2,1,0:T(2,128)(2,1)} %reshape.353), calls=%async_computation | async-start | bytes 524288 | tf_op jit(solution)/shard_map/all_to_all | solution.py:82
  23.3 8.0 %all-to-all-done = bf16[16,2,4096]{2,1,0:T(2,128)(2,1)S(1)} async-done(((bf16[16,2,4096]{2,1,0:T(2,128)(2,1)}), bf16[16,2,4096]{2,1,0:T(2,128)(2,1)S(1)}, u32[]{:S(2)}, u32[]{:S(2)}) %all-to-all-start) | async-done | bytes 262176 | tf_op jit(solution)/shard_map/all_to_all | solution.py:82
  42.2 3.5 %all-to-all-start.1 = ((bf16[16,1,64,128]{3,2,1,0:T(8,128)(2,1)}), bf16[16,1,64,128]{3,2,1,0:T(8,128)(2,1)S(1)}, u32[]{:S(2)}, u32[]{:S(2)}) async-start(bf16[16,1,64,128]{3,2,1,0:T(8,128)(2,1)} %get-tuple-element.21), calls=%async_computation.1 | async-start | bytes 524288 | tf_op jit(solution)/shard_map/all_to_all | solution.py:17
  45.8 1.7 broadcast_select_fusion
  48.4 7.4 %all-to-all-done.1 = bf16[16,1,64,128]{3,2,1,0:T(8,128)(2,1)S(1)} async-done(((bf16[16,1,64,128]{3,2,1,0:T(8,128)(2,1)}), bf16[16,1,64,128]{3,2,1,0:T(8,128)(2,1)S(1)}, u32[]{:S(2)}, u32[]{:S(2)}) %all-to-all-start.1) | async-done | bytes 262176 | tf_op jit(solution)/shard_map/all_to_all | solution.py:17
  55.7 3.5 %all-to-all-start.2 = ((bf16[16,1,64,128]{3,2,1,0:T(8,128)(2,1)}), bf16[16,1,64,128]{3,2,1,0:T(8,128)(2,1)S(1)}, u32[]{:S(2)}, u32[]{:S(2)}) async-start(bf16[16,1,64,128]{3,2,1,0:T(8,128)(2,1)} %get-tuple-element.22), calls=%async_computation.2 | async-start | bytes 524288 | tf_op jit(solution)/shard_map/all_to_all | solution.py:17
  59.6 0.8 constant_dynamic-slice_fusion
  60.9 11.2 %all-to-all-done.2 = bf16[16,1,64,128]{3,2,1,0:T(8,128)(2,1)S(1)} async-done(((bf16[16,1,64,128]{3,2,1,0:T(8,128)(2,1)}), bf16[16,1,64,128]{3,2,1,0:T(8,128)(2,1)S(1)}, u32[]{:S(2)}, u32[]{:S(2)}) %all-to-all-start.2) | async-done | bytes 262176 | tf_op jit(solution)/shard_map/all_to_all | solution.py:17
  72.1 1.4 stack.19
  73.5 1.7 maximum_bitcast_fusion
  75.2 2.2 gather_fusion.1
  77.4 2.7 %copy.60 = bf16[64,2,64,32]{2,3,1,0:T(8,128)(2,1)} copy(bf16[64,2,64,32]{3,2,1,0:T(8,128)(2,1)} %gather_fusion.1) | data formatting | bytes 1048576 | tf_op jit(solution)/shard_map/jit(_take)/gather | solution.py:100
  80.1 4.9 %fusion.9 = bf16[2,1,32,32,768]{4,3,0,2,1:T(8,128)(2,1)S(1)} fusion(bf16[32,2,64,768]{3,2,1,0:T(8,128)(2,1)} %param.7, bf16[32,2,2,64,32]{3,4,2,1,0:T(8,128)(2,1)} %bitcast.155, pred[32,2]{1,0:T(8,128)(4,1)S(1)} %copy.54), kind=kOutput, calls=%fused_computation.12 | convolution fusion | flops 404488192 | bytes 9961536 | tf_op jit(solution)/shard_map/tkcjoy,cjox->tkcyx/dot_general | solution.py:101
  85.0 7.2 %reshape.352 = bf16[2,32,32,12,64]{4,3,2,0,1:T(8,128)(2,1)} reshape(bf16[2,1,32,32,768]{4,3,0,2,1:T(8,128)(2,1)S(1)} %fusion.9) | data formatting | bytes 6291456 | tf_op jit(solution)/shard_map/reshape.88
  92.2 5.1 %fusion.6 = f32[2,1,32,12,32,128]{5,4,3,0,2,1:T(8,128)S(1)} fusion(bf16[32,64,128,1,1]{2,1,4,3,0:T(8,128)(2,1)} %bitcast.160, bf16[2,32,32,12,64]{4,3,2,0,1:T(8,128)(2,1)} %reshape.352), kind=kOutput, calls=%fused_computation.11 | convolution fusion | flops 402653184 | bytes 16252928 | tf_op jit(solution)/shard_map/kcix,tkcyai->tkcayx/dot_general | solution.py:107
  97.3 3.7 %fusion = (bf16[2,1,32,12,16,64]{5,4,3,0,2,1:T(8,128)(2,1)S(1)}, bf16[2,1,32,12,16,64]{5,4,3,0,2,1:T(8,128)(2,1)S(1)}) fusion(f32[2,1,32,12,32,128]{5,4,3,0,2,1:T(8,128)S(1)} %fusion.6), kind=kLoop, calls=%fused_computation.3 | loop fusion | flops 3145728 | bytes 15728640 | tf_op jit(solution)/shard_map/convert.6
  102.3 2.1 fusion.17
  104.4 1.6 collective-permute-start
  105.9 1.7 fusion.14
  107.7 0.7 slice_negate_fusion
  108.3 2.0 pad_maximum_fusion.2
  111.0 2.1 pad_maximum_fusion
  113.0 42.1 %all-reduce.3.cloned.1.call-done = (bf16[1,384,1536]{2,1,0:T(8,128)(2,1)}, bf16[1,384,1536]{2,1,0:T(8,128)(2,1)}) async-done(((bf16[1,384,1536]{2,1,0:T(8,128)(2,1)}, bf16[1,384,1536]{2,1,0:T(8,128)(2,1)}), (bf16[1,384,1536]{2,1,0:T(8,128)(2,1)}, bf16[1,384,1536]{2,1,0:T(8,128)(2,1)})) %all-reduce.3.cloned.1.call-update) | async-done | bytes 2359312 | tf_op jit(solution)/shard_map/psum | solution.py:23
  155.2 1.4 constant_dynamic-update-slice_fusion.33
  156.9 1.3 fusion.20
  158.3 0.8 copy-done.4
  159.2 2.5 %fusion.11 = bf16[1,384,2048]{1,2,0:T(8,128)(2,1)} fusion(f32[2048,384]{1,0:T(8,128)S(1)} %fusion.20, bf16[48,8,16,128]{3,2,1,0:T(8,128)(2,1)S(1)} %bitcast.157, bf16[2,384,1536]{2,1,0:T(8,128)(2,1)S(1)} %constant_dynamic-update-slice_fusion.32, s32[]{:T(128)S(6)} %select_n.104, s32[]{:T(128)S(6)} %select_n.98), kind=kOutput, calls=%fused_computation.23 | convolution fusion | flops 605552640 | bytes 6586376 | tf_op jit(solution)/shard_map/ab,kbx->kax/dot_general | solution.py:43
  161.6 2.6 %copy.69 = bf16[1,384,2048]{2,1,0:T(8,128)(2,1)} copy(bf16[1,384,2048]{1,2,0:T(8,128)(2,1)} %fusion.11) | data formatting | bytes 3145728 | tf_op jit(solution)/shard_map/convert_element_type | solution.py:132
  164.3 3.7 %convert_element_type.101 = bf16[6144,128]{1,0:T(8,128)(2,1)} reshape(bf16[1,384,2048]{2,1,0:T(8,128)(2,1)} %copy.69) | data formatting | bytes 3145728 | tf_op jit(solution)/shard_map/convert_element_type | solution.py:132
  168.0 2.3 %fusion.30 = f32[2048,384]{1,0:T(8,128)S(1)} fusion(bf16[48,8,16,128]{3,2,1,0:T(8,128)(2,1)S(1)} %bitcast.144, bf16[2,384,1536]{2,1,0:T(8,128)(2,1)} %copy-done.5, s32[]{:T(128)S(6)} %select_n.94, s32[]{:T(128)S(6)} %select_n.96), kind=kOutput, calls=%fused_computation.41 | convolution fusion | flops 603979776 | bytes 5013512 | tf_op jit(solution)/shard_map/ab,kbx->kax/dot_general | solution.py:42
  170.3 2.7 %slice_negate_fusion.1 = (bf16[1,384,16,64]{3,2,1,0:T(8,128)(2,1)S(1)}, bf16[1,384,16,64]{3,2,1,0:T(8,128)(2,1)S(1)}) fusion(bf16[1,384,16,128]{3,2,1,0:T(8,128)(2,1)} %bitcast.29), kind=kLoop, calls=%fused_computation.45 | loop fusion | flops 393216 | bytes 3145728 | tf_op jit(solution)/shard_map/neg | solution.py:33
  172.9 0.9 pad_maximum_fusion.1
  173.8 2.2 %fusion.23 = f32[2048,384]{1,0:T(8,128)S(1)} fusion(bf16[48,8,16,128]{3,2,1,0:T(8,128)(2,1)S(1)} %bitcast.154, bf16[2,384,1536]{2,1,0:T(8,128)(2,1)} %copy-done.5, s32[]{:T(128)S(6)} %select_n.94, s32[]{:T(128)S(6)} %select_n.103), kind=kOutput, calls=%fused_computation.34 | convolution fusion | flops 603979776 | bytes 5013512 | tf_op jit(solution)/shard_map/ab,kbx->kax/dot_general | solution.py:43
  176.0 2.8 %convolution_add_fusion = f32[2048,384]{1,0:T(8,128)S(1)} fusion(f32[2048,384]{1,0:T(8,128)S(1)} %fusion.23, bf16[48,8,16,128]{3,2,1,0:T(8,128)(2,1)} %bitcast.70, bf16[2,384,1536]{2,1,0:T(8,128)(2,1)} %copy-done.5, s32[]{:T(128)S(6)} %select_n.94, s32[]{:T(128)S(6)} %select_n.101), kind=kOutput, calls=%fused_computation.17 | convolution fusion | flops 604766208 | bytes 8159240 | tf_op jit(solution)/shard_map/ab,kbx->kax/dot_general | solution.py:42
  178.8 1.4 convert_bitcast_fusion
  180.8 3.6 %fusion.10 = bf16[1,384,2048]{1,2,0:T(8,128)(2,1)} fusion(f32[2048,384]{1,0:T(8,128)S(1)} %convolution_add_fusion, f32[2048,384]{1,0:T(8,128)S(1)} %fusion.30, bf16[48,8,16,128]{3,2,1,0:T(8,128)(2,1)S(1)} %bitcast.156, bf16[2,384,1536]{2,1,0:T(8,128)(2,1)} %copy-done.5, s32[]{:T(128)S(6)} %select_n.94, s32[]{:T(128)S(6)} %select_n.98), kind=kOutput, calls=%fused_computation.22 | convolution fusion | flops 606339072 | bytes 9732104 | tf_op jit(solution)/shard_map/ab,kbx->kax/dot_general | solution.py:43
  184.4 2.7 %copy.68 = bf16[1,384,2048]{2,1,0:T(8,128)(2,1)} copy(bf16[1,384,2048]{1,2,0:T(8,128)(2,1)} %fusion.10) | data formatting | bytes 3145728 | tf_op jit(solution)/shard_map/convert_element_type | solution.py:129
  187.1 3.7 %convert_element_type.97 = bf16[6144,128]{1,0:T(8,128)(2,1)} reshape(bf16[1,384,2048]{2,1,0:T(8,128)(2,1)} %copy.68) | data formatting | bytes 3145728 | tf_op jit(solution)/shard_map/convert_element_type | solution.py:129
  190.8 2.6 %copy.70 = bf16[1,384,2048]{2,1,0:T(8,128)(2,1)} copy(bf16[1,384,2048]{1,2,0:T(8,128)(2,1)} %convert_bitcast_fusion) | data formatting | bytes 3145728 | tf_op jit(solution)/shard_map/convert_element_type | solution.py:135
  193.4 3.8 %convert_element_type.105 = bf16[6144,128]{1,0:T(8,128)(2,1)} reshape(bf16[1,384,2048]{2,1,0:T(8,128)(2,1)} %copy.70) | data formatting | bytes 3145728 | tf_op jit(solution)/shard_map/convert_element_type | solution.py:135
  197.2 2.1 fusion.64
  200.0 0.8 copy-done.2
  201.5 0.7 fusion.54
  202.2 9.4 %reduce-scatter.2.cloned.1.call-done = bf16[1,32,128]{2,1,0:T(8,128)(2,1)} async-done(((bf16[1,64,128]{2,1,0:T(8,128)(2,1)}), bf16[1,32,128]{2,1,0:T(8,128)(2,1)}) %reduce-scatter.2.cloned.1.call-update) | async-done | bytes 8208 | tf_op jit(solution)/shard_map/reduce_scatter | solution.py:143
  211.6 1.3 convert_element_type.107
  (70 shorter events, 19.8 us)
Async XLA Ops:
  9.7 11.6 %copy-start.9 = (s32[2,16]{1,0:T(2,128)S(1)}, s32[2,16]{1,0:T(2,128)}, u32[]{:S(2)}) copy-start(s32[2,16]{1,0:T(2,128)} %param.10) | copy-start | bytes 388
  9.8 11.7 %copy-start.8 = (s32[2]{0:T(128)S(1)}, s32[2]{0:T(128)}, u32[]{:S(2)}) copy-start(s32[2]{0:T(128)} %param.11) | copy-start | bytes 28
  13.9 17.4 %all-to-all-start = ((bf16[16,2,4096]{2,1,0:T(2,128)(2,1)}), bf16[16,2,4096]{2,1,0:T(2,128)(2,1)S(1)}, u32[]{:S(2)}, u32[]{:S(2)}) async-start(bf16[16,2,4096]{2,1,0:T(2,128)(2,1)} %reshape.353), calls=%async_computation | async-start | bytes 524288 | tf_op jit(solution)/shard_map/all_to_all | solution.py:82
  32.3 13.5 %copy-start.7 = (bf16[1,384,1536]{2,1,0:T(8,128)(2,1)S(1)}, bf16[1,384,1536]{2,1,0:T(8,128)(2,1)}, u32[]{:S(2)}) copy-start(bf16[1,384,1536]{2,1,0:T(8,128)(2,1)} %param.9) | copy-start | bytes 3538948
  42.2 13.5 %all-to-all-start.1 = ((bf16[16,1,64,128]{3,2,1,0:T(8,128)(2,1)}), bf16[16,1,64,128]{3,2,1,0:T(8,128)(2,1)S(1)}, u32[]{:S(2)}, u32[]{:S(2)}) async-start(bf16[16,1,64,128]{3,2,1,0:T(8,128)(2,1)} %get-tuple-element.21), calls=%async_computation.1 | async-start | bytes 524288 | tf_op jit(solution)/shard_map/all_to_all | solution.py:17
  45.8 109.4 %all-reduce.3.cloned.1.call-start = ((), (), s32[]{:S(2)}) async-start(), calls=%async_computation.5 | async-start | bytes 4718592 | tf_op jit(solution)/shard_map/psum | solution.py:23
  47.5 0.7 copy-start.10
  47.5 12.1 %copy-start = (bf16[1,4096,128]{2,1,0:T(8,128)(2,1)S(1)}, bf16[1,4096,128]{2,1,0:T(8,128)(2,1)}, u32[]{:S(2)}) copy-start(bf16[1,4096,128]{2,1,0:T(8,128)(2,1)} %param.6) | copy-start | bytes 3145732
  55.7 16.4 %all-to-all-start.2 = ((bf16[16,1,64,128]{3,2,1,0:T(8,128)(2,1)}), bf16[16,1,64,128]{3,2,1,0:T(8,128)(2,1)S(1)}, u32[]{:S(2)}, u32[]{:S(2)}) async-start(bf16[16,1,64,128]{3,2,1,0:T(8,128)(2,1)} %get-tuple-element.22), calls=%async_computation.2 | async-start | bytes 524288 | tf_op jit(solution)/shard_map/all_to_all | solution.py:17
  59.3 152.3 %reduce-scatter.2.cloned.1.call-start = ((), (), s32[]{:S(2)}) async-start(), calls=%async_computation.4 | async-start | bytes 24576 | tf_op jit(solution)/shard_map/reduce_scatter | solution.py:143
  104.4 65.9 %collective-permute-start = (bf16[1,1,384,16,128]{4,3,2,1,0:T(8,128)(2,1)}, bf16[1,1,384,16,128]{4,3,2,1,0:T(8,128)(2,1)}, u32[]{:S(2)}, u32[]{:S(2)}) collective-permute-start(bf16[1,1,384,16,128]{4,3,2,1,0:T(8,128)(2,1)} %fusion.17), channel_id=1, source_target_pairs={{0,1},{1,0},{2,3},{3,2},{4,5},{5,4},{6,7},{7,6},{8,9},{9,8},{10,11... | collective-permute-start | bytes 4718600 | tf_op jit(solution)/shard_map/ppermute | solution.py:29
  155.2 1.6 copy-start.6
  156.9 1.4 copy-start.5
  156.9 2.3 %copy-start.4 = (bf16[1,384,16,128]{3,2,1,0:T(8,128)(2,1)S(1)}, bf16[1,384,16,128]{3,2,1,0:T(8,128)(2,1)}, u32[]{:S(2)}) copy-start(bf16[1,384,16,128]{3,2,1,0:T(8,128)(2,1)} %pad_maximum_fusion.2) | copy-start | bytes 4718596
  178.8 2.0 copy-start.1
  197.2 2.1 copy-start.3
  199.4 1.4 copy-start.2
Sparse Core Ops, SparseCore 0:
  50.2 104.9 all-reduce.2
  202.3 9.2 reduce-scatter.1
